TPU v7x, 256 devices: a whole 4x4x8 slice. The times are simulated.
256 devices in a mesh: tok: 8 (over z), tp: 16 (over y, x), grp: 2 (over core).
Axes of the slice: x: 4, y: 4, z: 8, core: 2. Of those that a mesh axis runs over, the one named last changes fastest.
Arguments:
- hidden: bfloat16 [2048, 6144], P(('tok', 'grp'), 'tp'), may hold values from -6 to 6
- gain: bfloat16 [6144], P('tp'), may hold values from 0.5 to 1.5
- expert_ids: int32 [2048, 2], P(('tok', 'grp')), may hold values from 0 to 7, all different within a row; in each aligned block of 128 rows (0 to 127, 128 to 255, ...) at most 40 rows name the same one
- gate_weights: float32 [2048, 2], P(('tok', 'grp')), may hold values from 0.1 to 0.9
- segment_ids: int32 [2048], P(('tok', 'grp')), may hold values from 0 to 15, never falling along the last dimension, each value on 1 to 384 neighbouring positions
- upstream: bfloat16 [2048, 6144], P(('tok', 'grp'), 'tp'), may hold values from -6 to 6
- w_gate: bfloat16 [8, 6144, 8192], P('tok', None, ('tp', 'grp')), may hold values from -0.078125 to 0.078125
- w_up: bfloat16 [8, 6144, 8192], P('tok', None, ('tp', 'grp')), may hold values from -0.078125 to 0.078125
- w_down: bfloat16 [8, 8192, 6144], P('tok', ('tp', 'grp')), may hold values from -0.0625 to 0.0625
Outputs:
- mixed: bfloat16 [2048, 6144], P(('tok', 'grp'), 'tp')
- importance: float32 [8, 8192], P('tok', ('tp', 'grp'))
Inputs may be any that keep to these rules, and one draw needn't show every extreme that they name: `expert_ids`: each token names 2 different experts. Within the tokens of one token shard (aligned blocks of 128 rows) no expert is named by more than 40 tokens, and in some block one expert is named by exactly 40. `segment_ids`: never falling along the tokens; every document holds between 1 and 384 tokens.
All inputs are finite; a program needn't handle non-finite values.
Results may differ from a plain program's by a relative error of at most 0.0095.
Values may be sent and summed in bfloat16 or wider, within the bound.
No kernel may reach another device: no remote copies, remote signals or barrier semaphores. Data moves between devices by JAX's collectives and lax.ppermute only.
A program may use at most 128 MiB of HBM per device.

v0:
```python
import jax
import jax.numpy as jnp
from jax import lax
from jax.sharding import PartitionSpec as P


def expert_pass(rows_in, cot_in, gate_mat, up_mat, down_mat):
    gate_pre = jnp.dot(rows_in, gate_mat, preferred_element_type=jnp.float32)
    up_proj = jnp.dot(rows_in, up_mat, preferred_element_type=jnp.float32)
    sigmoid_gate = jax.nn.sigmoid(gate_pre)
    activated = gate_pre * sigmoid_gate
    hidden_act = (activated * up_proj).astype(jnp.bfloat16)
    grad_act = lax.dot_general(
        cot_in, down_mat, (((1,), (1,)), ((), ())), preferred_element_type=jnp.float32
    )
    grad_gate = (
        grad_act * up_proj * sigmoid_gate * (1.0 + gate_pre * (1.0 - sigmoid_gate))
    ).astype(jnp.bfloat16)
    grad_up = (grad_act * activated).astype(jnp.bfloat16)
    grad_wgate = lax.dot_general(
        rows_in, grad_gate, (((0,), (0,)), ((), ())), preferred_element_type=jnp.float32
    )
    grad_wup = lax.dot_general(
        rows_in, grad_up, (((0,), (0,)), ((), ())), preferred_element_type=jnp.float32
    )
    grad_wdown = lax.dot_general(
        hidden_act, cot_in, (((0,), (0,)), ((), ())), preferred_element_type=jnp.float32
    )
    scores = jnp.sum(jnp.abs(grad_wgate * gate_mat.astype(jnp.float32)), axis=0)
    scores = scores + jnp.sum(jnp.abs(grad_wup * up_mat.astype(jnp.float32)), axis=0)
    scores = scores + jnp.sum(jnp.abs(grad_wdown * down_mat.astype(jnp.float32)), axis=1)
    return (hidden_act, scores)


def on_device(hidden, gain, expert_ids, gate_weights, segment_ids, upstream, w_gate, w_up, w_down):
    rows_here = hidden.shape[0]
    top_count = expert_ids.shape[1]
    experts = lax.axis_size("tok")
    groups = lax.axis_size("grp")
    capacity = 5 * rows_here // (2 * experts)
    width = w_gate.shape[1]
    documents = jnp.arange(experts * groups, dtype=jnp.int32)
    doc_onehot = (segment_ids[:, None] == documents[None, :]).astype(jnp.float32)
    doc_len = lax.psum(jnp.sum(doc_onehot, axis=0), ("tok", "grp"))
    tok_len = jnp.sum(doc_onehot * doc_len[None, :], axis=1)
    tok_weight = rows_here / tok_len
    onehot = (
        expert_ids.reshape(-1)[:, None] == jnp.arange(experts, dtype=jnp.int32)[None, :]
    ).astype(jnp.int32)
    before = jnp.cumsum(onehot, axis=0) - onehot
    slot_ids = jnp.sum(before * onehot, axis=1).reshape(rows_here, top_count)
    targets = expert_ids * capacity + slot_ids
    all_slots = jnp.arange(experts * capacity, dtype=jnp.int32)
    matches = all_slots[:, None, None] == targets[None, :, :]
    placing = jnp.any(matches, axis=2).astype(jnp.bfloat16)
    scaled = gate_weights * tok_weight[:, None]
    slot_scale = jnp.sum(jnp.where(matches, scaled[None, :, :], 0.0), axis=(1, 2))
    combining = jnp.sum(jnp.where(matches, gate_weights[None, :, :], 0.0), axis=2)
    wide_hidden = hidden.astype(jnp.float32)
    squares = lax.psum(jnp.sum(wide_hidden * wide_hidden, axis=1), "tp")
    scaling = lax.rsqrt(squares / width + 1e-05)
    normed = (wide_hidden * scaling[:, None] * gain.astype(jnp.float32)[None, :]).astype(
        jnp.bfloat16
    )
    block_rows = jnp.dot(placing, normed, preferred_element_type=jnp.float32).astype(jnp.bfloat16)
    block_cot = jnp.dot(placing, upstream, preferred_element_type=jnp.float32) * slot_scale[:, None]
    block_rows = block_rows.reshape(experts, capacity, -1)
    block_cot = block_cot.astype(jnp.bfloat16).reshape(experts, capacity, -1)
    came_rows, came_cot = (
        lax.all_to_all(block_rows, "tok", split_axis=0, concat_axis=0, tiled=True),
        lax.all_to_all(block_cot, "tok", split_axis=0, concat_axis=0, tiled=True),
    )
    part_rows, part_cot = (
        lax.all_gather(came_rows, "tp", axis=2, tiled=True),
        lax.all_gather(came_cot, "tp", axis=2, tiled=True),
    )
    pooled_rows, pooled_cot = (
        lax.all_gather(part_rows, "grp", axis=0, tiled=True),
        lax.all_gather(part_cot, "grp", axis=0, tiled=True),
    )
    rows_in = pooled_rows.reshape(-1, width)
    cot_in = pooled_cot.reshape(-1, width)
    gate_mat = w_gate[0]
    up_mat = w_up[0]
    down_mat = w_down[0]
    hidden_act, scores = expert_pass(rows_in, cot_in, gate_mat, up_mat, down_mat)
    importance = scores / (rows_here * experts * groups)
    partial_value = lax.psum_scatter(
        lax.dot_general(
            down_mat, hidden_act, (((0,), (1,)), ((), ())), preferred_element_type=jnp.float32
        ).astype(jnp.bfloat16),
        "tp",
        scatter_dimension=0,
        tiled=True,
    )
    summed = lax.psum_scatter(partial_value, "grp", scatter_dimension=1, tiled=True).astype(
        jnp.float32
    )
    slice_width = summed.shape[0]
    outgoing = summed.astype(jnp.bfloat16).reshape(slice_width, experts, capacity)
    returned = lax.all_to_all(outgoing, "tok", split_axis=1, concat_axis=1, tiled=True)
    returned = returned.reshape(slice_width, experts * capacity).astype(jnp.float32)
    combined = lax.dot_general(
        combining,
        returned,
        (((0,), (1,)), ((), ())),
        precision=lax.Precision.HIGHEST,
        preferred_element_type=jnp.float32,
    )
    mixed = (hidden.astype(jnp.float32) + combined).astype(jnp.bfloat16)
    return (mixed, importance[None, :])


def solution(mesh):
    placed = (
        P(("tok", "grp"), "tp"),
        P("tp"),
        P(("tok", "grp"), None),
        P(("tok", "grp"), None),
        P(("tok", "grp")),
        P(("tok", "grp"), "tp"),
        P("tok", None, ("tp", "grp")),
        P("tok", None, ("tp", "grp")),
        P("tok", ("tp", "grp"), None),
    )
    return jax.shard_map(
        on_device,
        mesh=mesh,
        in_specs=placed,
        out_specs=(P(("tok", "grp"), "tp"), P("tok", ("tp", "grp"))),
        check_vma=False,
    )
```

profile of v0, /device:TPU:1, one launch (start us, length us, event | category | flops | bytes accessed | tf_op | source)
XLA Modules:
  0.0 378.7 jit_solution(2218602018310981666)
XLA Ops:
  7.2 0.9 copy.31
  8.2 0.1 eq.56
  8.3 0.1 eq.52
  8.5 1.0 fusion.19
  9.5 34.2 %psum.14 = f32[128]{0:T(128)S(1)} all-reduce(f32[128]{0:T(128)S(1)} %fusion.19), channel_id=1, replica_groups=mesh['tok'=8,'tp'=16,'grp'=2] {'tp'}, use_global_device_ids=true, to_apply=%region_6.7 | all-reduce | flops 128 | bytes 1024 | tf_op jit(solution)/shard_map/psum | solution.py:60
  43.7 0.7 convert_element_type.60
  44.4 0.6 reduce-window.6
  45.0 0.2 slice_reduce_fusion
  45.2 0.1 fusion.27
  45.3 0.1 reshape.79
  45.5 0.1 copy.33
  45.5 0.7 multiply_add_fusion
  46.3 1.2 convolution_convert_fusion.1
  47.5 17.2 %all_to_all.15 = bf16[8,40,384]{2,1,0:T(8,128)(2,1)} all-to-all(bf16[8,40,384]{2,1,0:T(8,128)(2,1)S(1)} %bitcast.56), channel_id=1, replica_groups=mesh['tok'=8,'tp'=16,'grp'=2] {'tok'}, dimensions={0} | all-to-all | bytes 491520 | tf_op jit(solution)/shard_map/all_to_all | solution.py:70
  64.7 0.0 all-gather.9.cloned.1.call-start
  64.8 0.8 convert_reduce_fusion
  65.6 32.2 %psum.15 = f32[16]{0:T(128)S(1)} all-reduce(f32[16]{0:T(128)S(1)} %convert_reduce_fusion), channel_id=1, replica_groups=mesh['tok'=8,'tp'=16,'grp'=2] {'tok','grp'}, use_global_device_ids=true, to_apply=%region_10.11 | all-reduce | flops 16 | bytes 128 | tf_op jit(solution)/shard_map/psum | solution.py:44
  97.8 0.7 select_reduce_fusion.2
  98.5 0.7 broadcast_multiply_fusion
  99.2 1.5 select_reduce_fusion
  100.7 0.2 fusion.14
  101.0 12.8 %all_to_all.16 = bf16[8,40,384]{2,1,0:T(8,128)(2,1)} all-to-all(bf16[8,40,384]{2,1,0:T(8,128)(2,1)S(1)} %bitcast.57), channel_id=1, replica_groups=mesh['tok'=8,'tp'=16,'grp'=2] {'tok'}, dimensions={0} | all-to-all | bytes 491520 | tf_op jit(solution)/shard_map/all_to_all | solution.py:71
  113.8 0.0 all-gather.7.cloned.1.call-start
  113.8 10.2 %all-gather.5.cloned.1.call-done = bf16[8,40,6144]{2,1,0:T(8,128)(2,1)} async-done(((bf16[8,40,384]{2,1,0:T(8,128)(2,1)}), bf16[8,40,6144]{2,1,0:T(8,128)(2,1)}) %all-gather.5.cloned.1.call-update) | async-done | bytes 3932176 | tf_op jit(solution)/shard_map/all_gather | solution.py:74
  124.1 0.0 all-gather.11.cloned.1.call-start
  124.1 62.4 %all-gather.9.cloned.1.call-done = bf16[8,40,6144]{2,1,0:T(8,128)(2,1)} async-done(((bf16[8,40,384]{2,1,0:T(8,128)(2,1)}), bf16[8,40,6144]{2,1,0:T(8,128)(2,1)}) %all-gather.9.cloned.1.call-update) | async-done | bytes 3932176 | tf_op jit(solution)/shard_map/all_gather | solution.py:75
  186.5 0.0 reduce-scatter.7.cloned.1.call-start
  186.5 27.7 %all-gather.7.cloned.1.call-done = bf16[16,40,6144]{2,1,0:T(8,128)(2,1)} async-done(((bf16[8,40,6144]{2,1,0:T(8,128)(2,1)}), bf16[16,40,6144]{2,1,0:T(8,128)(2,1)}) %all-gather.7.cloned.1.call-update) | async-done | bytes 7864336 | tf_op jit(solution)/shard_map/all_gather | solution.py:78
  214.2 5.6 %fusion.9 = f32[640,256]{1,0:T(8,128)S(1)} fusion(bf16[640,6144]{1,0:T(8,128)(2,1)} %bitcast.60, bf16[1,6144,256]{2,1,0:T(8,128)(2,1)S(1)} %copy-done.4), kind=kOutput, calls=%fused_computation.13 | convolution fusion | flops 2013265920 | bytes 11665408 | tf_op jit(solution)/shard_map/dot_general | solution.py:8
  219.8 0.8 copy-done.6
  220.6 3.0 multiply_convert_fusion.2
  223.6 0.7 copy-done.2
  224.4 6.1 %fusion = bf16[6144,640]{0,1:T(8,128)(2,1)} fusion(bf16[640,256]{1,0:T(8,128)(2,1)S(1)} %get-tuple-element.4, bf16[1,256,6144]{2,1,0:T(8,128)(2,1)S(1)} %copy-done.1), kind=kOutput, calls=%fused_computation.1 | convolution fusion | flops 2017198080 | bytes 11337728 | tf_op jit(solution)/shard_map/dot_general | solution.py:89
  230.5 10.7 %copy.34 = bf16[6144,640]{1,0:T(8,128)(2,1)} copy(bf16[6144,640]{0,1:T(8,128)(2,1)} %fusion) | data formatting | bytes 15728640
  241.2 0.2 reduce-scatter.5.cloned.1.call-start
  241.5 0.1 all-gather.11.cloned.1.call-done
  241.6 5.6 %fusion.4 = f32[640,256]{1,0:T(8,128)S(1)} fusion(bf16[640,6144]{1,0:T(8,128)(2,1)} %bitcast.53, bf16[1,256,6144]{2,1,0:T(8,128)(2,1)S(1)} %copy-done.1), kind=kOutput, calls=%fused_computation.8 | convolution fusion | flops 2013265920 | bytes 11665408 | tf_op jit(solution)/shard_map/dot_general | solution.py:13
  247.2 0.8 copy-done.9
  248.1 6.2 %fusion.11 = f32[256]{0:T(256)S(1)} fusion(bf16[1,6144,256]{2,1,0:T(8,128)(2,1)S(1)} %copy-done.5, bf16[640,6144]{1,0:T(8,128)(2,1)} %bitcast.61, f32[640,256]{1,0:T(8,128)S(1)} %copy-done.8, f32[640,256]{1,0:T(8,128)S(1)} %fusion.4, f32[640,256]{1,0:T(8,128)S(1)} %copy-done.10), kind=kOutput, calls=%fused_computation.15 | convolution fusion | flops 2021195520 | bytes 12977152 | tf_op jit(solution)/shard_map/dot_general | solution.py:20
  254.3 80.1 %reduce-scatter.7.cloned.1.call-done = bf16[384,640]{1,0:T(8,128)(2,1)} async-done(((bf16[6144,640]{1,0:T(8,128)(2,1)}), bf16[384,640]{1,0:T(8,128)(2,1)}) %reduce-scatter.7.cloned.1.call-update) | async-done | bytes 491536
  334.4 2.0 copy.35
  336.5 7.4 %fusion.12 = f32[256]{0:T(256)S(1)} fusion(bf16[1,6144,256]{2,1,0:T(8,128)(2,1)} %param.16, bf16[640,6144]{1,0:T(8,128)(2,1)} %bitcast.62, f32[640,256]{1,0:T(8,128)} %copy-done.9, f32[640,256]{1,0:T(8,128)} %copy-done.7), kind=kOutput, calls=%fused_computation.16 | convolution fusion | flops 2020540160 | bytes 12321792 | tf_op jit(solution)/shard_map/dot_general | solution.py:23
  343.8 7.7 %reduce-scatter.5.cloned.1.call-done = bf16[384,320]{0,1:T(8,128)(2,1)} async-done(((bf16[384,640]{0,1:T(8,128)(2,1)}), bf16[384,320]{0,1:T(8,128)(2,1)}) %reduce-scatter.5.cloned.1.call-update) | async-done | bytes 245776 | tf_op jit(solution)/shard_map/reduce_scatter | solution.py:96
  351.5 6.5 %all-to-all-start.1 = ((bf16[384,8,40]{0,2,1:T(8,128)(2,1)}), bf16[384,8,40]{0,2,1:T(8,128)(2,1)S(1)}, u32[]{:S(2)}, u32[]{:S(2)}) async-start(bf16[384,8,40]{0,2,1:T(8,128)(2,1)} %bitcast.58), calls=%async_computation.2 | async-start | bytes 491520 | tf_op jit(solution)/shard_map/all_to_all | solution.py:101
  358.0 6.5 %fusion.13 = f32[256]{0:T(256)S(1)} fusion(bf16[1,256,6144]{2,1,0:T(8,128)(2,1)S(1)} %copy-done.1, bf16[640,256]{1,0:T(8,128)(2,1)} %copy-done.2, bf16[640,6144]{1,0:T(8,128)(2,1)} %bitcast.54), kind=kOutput, calls=%fused_computation.17 | convolution fusion | flops 2019557120 | bytes 11338752 | tf_op jit(solution)/shard_map/dot_general | solution.py:26
  364.5 0.6 add_multiply_fusion
  365.0 4.8 %all-to-all-done.1 = bf16[384,8,40]{0,2,1:T(8,128)(2,1)S(1)} async-done(((bf16[384,8,40]{0,2,1:T(8,128)(2,1)}), bf16[384,8,40]{0,2,1:T(8,128)(2,1)S(1)}, u32[]{:S(2)}, u32[]{:S(2)}) %all-to-all-start.1) | async-done | bytes 245792 | tf_op jit(solution)/shard_map/all_to_all | solution.py:101
  369.8 2.0 fusion.15
  (32 shorter events, 0.3 us)
Async XLA Ops:
  7.2 93.6 %copy-start = (bf16[128,384]{1,0:T(8,128)(2,1)S(1)}, bf16[128,384]{1,0:T(8,128)(2,1)}, u32[]{:S(2)}) copy-start(bf16[128,384]{1,0:T(8,128)(2,1)} %param.14) | copy-start | bytes 294916
  7.2 207.0 %copy-start.4 = (bf16[1,6144,256]{2,1,0:T(8,128)(2,1)S(1)}, bf16[1,6144,256]{2,1,0:T(8,128)(2,1)}, u32[]{:S(2)}) copy-start(bf16[1,6144,256]{2,1,0:T(8,128)(2,1)} %param.15) | copy-start | bytes 9437188
  7.2 116.8 %all-gather.5.cloned.1.call-start = ((), (), s32[]{:S(2)}) async-start(), calls=%async_computation.5 | async-start | bytes 4177920 | tf_op jit(solution)/shard_map/all_gather | solution.py:74
  64.7 121.7 %all-gather.9.cloned.1.call-start = ((), (), s32[]{:S(2)}) async-start(), calls=%async_computation.8 | async-start | bytes 4177920 | tf_op jit(solution)/shard_map/all_gather | solution.py:75
  113.8 100.4 %all-gather.7.cloned.1.call-start = ((), (), s32[]{:S(2)}) async-start(), calls=%async_computation.6 | async-start | bytes 11796480 | tf_op jit(solution)/shard_map/all_gather | solution.py:78
  124.1 117.6 %all-gather.11.cloned.1.call-start = ((), (), s32[]{:S(2)}) async-start(), calls=%async_computation.9 | async-start | bytes 11796480 | tf_op jit(solution)/shard_map/all_gather | solution.py:79
  186.5 147.9 %reduce-scatter.7.cloned.1.call-start = ((), (), s32[]{:S(2)}) async-start(), calls=%async_computation.10 | async-start | bytes 8355840
  214.2 5.6 %copy-start.3 = (bf16[16,40,6144]{2,1,0:T(8,128)(2,1)S(1)}, bf16[16,40,6144]{2,1,0:T(8,128)(2,1)}, u32[]{:S(2)}) copy-start(bf16[16,40,6144]{2,1,0:T(8,128)(2,1)} %all-gather.7.cloned.1.call-done) | copy-start | bytes 23592964
  214.2 6.4 %copy-start.6 = (bf16[1,6144,256]{2,1,0:T(8,128)(2,1)S(1)}, bf16[1,6144,256]{2,1,0:T(8,128)(2,1)}, u32[]{:S(2)}) copy-start(bf16[1,6144,256]{2,1,0:T(8,128)(2,1)} %param.16) | copy-start | bytes 9437188
  220.6 3.0 copy-start.7
  220.6 3.8 copy-start.1
  223.6 0.7 copy-start.2
  241.2 110.2 %reduce-scatter.5.cloned.1.call-start = ((), (), s32[]{:S(2)}) async-start(), calls=%async_computation.7 | async-start | bytes 737280 | tf_op jit(solution)/shard_map/reduce_scatter | solution.py:96
  241.6 6.5 %copy-start.5 = (bf16[1,6144,256]{2,1,0:T(8,128)(2,1)S(1)}, bf16[1,6144,256]{2,1,0:T(8,128)(2,1)}, u32[]{:S(2)}) copy-start(bf16[1,6144,256]{2,1,0:T(8,128)(2,1)} %param.15) | copy-start | bytes 9437188
  241.6 6.5 %copy-start.8 = (f32[640,256]{1,0:T(8,128)S(1)}, f32[640,256]{1,0:T(8,128)}, u32[]{:S(2)}) copy-start(f32[640,256]{1,0:T(8,128)} %copy-done.7) | copy-start | bytes 1966084
  241.6 6.5 %copy-start.10 = (f32[640,256]{1,0:T(8,128)S(1)}, f32[640,256]{1,0:T(8,128)}, u32[]{:S(2)}) copy-start(f32[640,256]{1,0:T(8,128)} %get-tuple-element.5) | copy-start | bytes 1966084
  247.2 0.8 copy-start.9
  351.5 18.3 %all-to-all-start.1 = ((bf16[384,8,40]{0,2,1:T(8,128)(2,1)}), bf16[384,8,40]{0,2,1:T(8,128)(2,1)S(1)}, u32[]{:S(2)}, u32[]{:S(2)}) async-start(bf16[384,8,40]{0,2,1:T(8,128)(2,1)} %bitcast.58), calls=%async_computation.2 | async-start | bytes 491520 | tf_op jit(solution)/shard_map/all_to_all | solution.py:101
Sparse Core Ops, SparseCore 0:
  64.9 59.1 all-gather.4
  126.4 59.9 all-gather.8
  188.3 25.9 all-gather.6
  215.9 25.6 all-gather.10
  245.3 89.1 reduce-scatter.6
  336.8 14.6 reduce-scatter.4
where the time goes:
time: 379 us
  waiting for transfers between devices  193 us (51%)
  blocking collectives  96.5 us (25%)
  matrix products  43.9 us (12%)
  local copies, waits for them, and re-layouts  16.8 us (4%)
  between operations  14.2 us (4%)
  other arithmetic  7.42 us (2%)
  starting transfers between devices  6.89 us (2%)
    unnamed x7, waiting for transfers between devices  80.2 us
    all_gather x1, waiting for transfers between devices, on_device(): lax.all_gather(came_cot, 'tp', axis=2, tiled=True)  62.4 us
    psum x1, blocking collectives, on_device(): squares = lax.psum(jnp.sum(wide_hidden * wide_hidden, axis=1), 'tp')  34.2 us
    psum x1, blocking collectives, on_device(): doc_len = lax.psum(jnp.sum(doc_onehot, axis=0), ('tok', 'grp'))  32.2 us
    all_gather x1, waiting for transfers between devices, on_device(): lax.all_gather(part_rows, 'grp', axis=0, tiled=True)  27.7 us
    all_to_all x1, blocking collectives, on_device(): lax.all_to_all(block_rows, 'tok', split_axis=0, concat_axis=0, tiled=True)  17.2 us
    unnamed x25, local copies, waits for them, and re-layouts  16.1 us
    all_to_all x1, blocking collectives, on_device(): lax.all_to_all(block_cot, 'tok', split_axis=0, concat_axis=0, tiled=True)  12.8 us
  transfers between devices with their start and end apart: 7, of which 7 were waited for; matrix products, arithmetic and copies ran while one was open for 15% of the time, Pallas kernels for 0%

commit v1 on v0

--- a/solution.py
+++ b/solution.py
@@ -74,8 +74,17 @@
         lax.all_gather(came_rows, "tp", axis=2, tiled=True),
         lax.all_gather(came_cot, "tp", axis=2, tiled=True),
     )
+
+    def shards_bring(my_data, mesh_ax):
+        return jnp.concatenate(
+            lax.all_to_all(
+                jnp.stack([my_data for _ in range(lax.axis_size(mesh_ax))], 0), mesh_ax, 0, 0
+            ),
+            0,
+        )
+
     pooled_rows, pooled_cot = (
-        lax.all_gather(part_rows, "grp", axis=0, tiled=True),
+        shards_bring(part_rows, "grp"),
         lax.all_gather(part_cot, "grp", axis=0, tiled=True),
     )
     rows_in = pooled_rows.reshape(-1, width)

time: 379 us -> 349 us (0.921)
  waiting for transfers between devices: 193 us -> 158 us
  matrix products: 43.9 us -> 39.8 us
  other arithmetic: 7.42 us -> 11.5 us
    all_gather x1, waiting for transfers between devices: 62.4 us -> 8.77 us  [on_device(): lax.all_gather(came_cot, 'tp', axis=2, tiled=True)]
    all_gather x1, waiting for transfers between devices: 10.2 us -> 62.4 us  [on_device(): lax.all_gather(came_rows, 'tp', axis=2, tiled=True)]
    all_gather x1 -> x0, waiting for transfers between devices: 27.7 us -> none  [on_device(): lax.all_gather(part_rows, 'grp', axis=0, tiled=True)]
    all_to_all x0 -> x1, blocking collectives: none -> 12 us  [shards_bring(): lax.all_to_all(jnp.stack([my_data for _ in range(lax.axis_size(mesh_ax))]...]
    unnamed x7 -> x6, waiting for transfers between devices: 80.2 us -> 74.6 us
    all_to_all x1, blocking collectives: 17.2 us -> 12.2 us  [on_device(): lax.all_to_all(block_rows, 'tok', split_axis=0, concat_axis=0, tiled=True)]
    psum x1, blocking collectives: 32.2 us -> 27.4 us  [on_device(): doc_len = lax.psum(jnp.sum(doc_onehot, axis=0), ('tok', 'grp'))]
    another operation x2 -> x3, other arithmetic: 0.61 us -> 4.67 us  [the longest x1 4.05 us: shards_bring(): jnp.stack([my_data for _ in range(lax.axis_size(mesh_ax))], 0)]
  transfers between devices with their start and end apart: 7 -> 6, of which waited for: 7 -> 5; matrix products, arithmetic and copies ran while one was open for 15% -> 16% of each run, Pallas kernels for 0% -> 0%
where the time goes in v1:
time: 349 us
  waiting for transfers between devices  158 us (45%)
  blocking collectives  100 us (29%)
  matrix products  39.8 us (11%)
  local copies, waits for them, and re-layouts  18.1 us (5%)
  between operations  13.9 us (4%)
  other arithmetic  11.5 us (3%)
  starting transfers between devices  6.84 us (2%)
    unnamed x6, waiting for transfers between devices  74.6 us
    all_gather x1, waiting for transfers between devices, on_device(): lax.all_gather(came_rows, 'tp', axis=2, tiled=True)  62.4 us
    psum x1, blocking collectives, on_device(): squares = lax.psum(jnp.sum(wide_hidden * wide_hidden, axis=1), 'tp')  33.4 us
    psum x1, blocking collectives, on_device(): doc_len = lax.psum(jnp.sum(doc_onehot, axis=0), ('tok', 'grp'))  27.4 us
    unnamed x25, local copies, waits for them, and re-layouts  17.4 us
    all_to_all x1, blocking collectives, on_device(): lax.all_to_all(block_cot, 'tok', split_axis=0, concat_axis=0, tiled=True)  15.2 us
    all_to_all x1, blocking collectives, on_device(): lax.all_to_all(block_rows, 'tok', split_axis=0, concat_axis=0, tiled=True)  12.2 us
    all_to_all x1, blocking collectives, shards_bring(): lax.all_to_all(jnp.stack([my_data for _ in range(lax.axis_size(mesh_ax))]...  12 us
  transfers between devices with their start and end apart: 6, of which 5 were waited for; matrix products, arithmetic and copies ran while one was open for 16% of the time, Pallas kernels for 0%

profile of v1, /device:TPU:1, one launch (start us, length us, event | category | flops | bytes accessed | tf_op | source)
XLA Modules:
  0.0 348.5 jit_solution(8825221306228375005)
XLA Ops:
  7.2 0.8 copy.31
  8.0 0.1 eq.56
  8.2 0.1 eq.52
  8.3 0.6 reduce-window.6
  8.9 0.2 slice_reduce_fusion
  9.1 0.1 fusion.27
  9.2 0.1 reshape.76
  9.4 0.1 copy.33
  9.5 0.7 multiply_add_fusion
  10.2 0.8 convert_reduce_fusion
  11.0 27.4 %psum.15 = f32[16]{0:T(128)S(1)} all-reduce(f32[16]{0:T(128)S(1)} %convert_reduce_fusion), channel_id=1, replica_groups=mesh['tok'=8,'tp'=16,'grp'=2] {'tok','grp'}, use_global_device_ids=true, to_apply=%region_10.11 | all-reduce | flops 16 | bytes 128 | tf_op jit(solution)/shard_map/psum | solution.py:44
  38.4 0.7 select_reduce_fusion.2
  39.1 0.7 broadcast_multiply_fusion
  39.8 1.5 select_reduce_fusion
  41.3 0.2 fusion.14
  41.5 15.2 %all_to_all.20 = bf16[8,40,384]{2,1,0:T(8,128)(2,1)} all-to-all(bf16[8,40,384]{2,1,0:T(8,128)(2,1)S(1)} %bitcast.63), channel_id=1, replica_groups=mesh['tok'=8,'tp'=16,'grp'=2] {'tok'}, dimensions={0} | all-to-all | bytes 491520 | tf_op jit(solution)/shard_map/all_to_all | solution.py:71
  56.7 0.0 all-gather.4.cloned.1.call-start
  56.8 0.7 convert_element_type.60
  57.5 1.0 fusion.19
  58.5 33.4 %psum.14 = f32[128]{0:T(128)S(1)} all-reduce(f32[128]{0:T(128)S(1)} %fusion.19), channel_id=1, replica_groups=mesh['tok'=8,'tp'=16,'grp'=2] {'tp'}, use_global_device_ids=true, to_apply=%region_6.7 | all-reduce | flops 128 | bytes 1024 | tf_op jit(solution)/shard_map/psum | solution.py:60
  91.9 1.2 convolution_convert_fusion.1
  93.1 12.2 %all_to_all.21 = bf16[8,40,384]{2,1,0:T(8,128)(2,1)} all-to-all(bf16[8,40,384]{2,1,0:T(8,128)(2,1)S(1)} %bitcast.62), channel_id=1, replica_groups=mesh['tok'=8,'tp'=16,'grp'=2] {'tok'}, dimensions={0} | all-to-all | bytes 491520 | tf_op jit(solution)/shard_map/all_to_all | solution.py:70
  105.3 0.0 all-gather.8.cloned.1.call-start
  105.4 8.8 %all-gather.6.cloned.1.call-done = bf16[8,40,6144]{2,1,0:T(8,128)(2,1)} async-done(((bf16[8,40,384]{2,1,0:T(8,128)(2,1)}), bf16[8,40,6144]{2,1,0:T(8,128)(2,1)}) %all-gather.6.cloned.1.call-update) | async-done | bytes 3932176 | tf_op jit(solution)/shard_map/all_gather | solution.py:75
  114.2 0.0 reduce-scatter.7.cloned.1.call-start
  114.2 62.4 %all-gather.4.cloned.1.call-done = bf16[8,40,6144]{2,1,0:T(8,128)(2,1)} async-done(((bf16[8,40,384]{2,1,0:T(8,128)(2,1)}), bf16[8,40,6144]{2,1,0:T(8,128)(2,1)}) %all-gather.4.cloned.1.call-update) | async-done | bytes 3932176 | tf_op jit(solution)/shard_map/all_gather | solution.py:74
  176.6 4.0 %pad_maximum_fusion = bf16[2,8,40,6144]{3,2,1,0:T(8,128)(2,1)S(1)} fusion(bf16[1,8,40,6144]{3,2,1,0:T(8,128)(2,1)} %bitcast.60), kind=kLoop, calls=%fused_computation.8 | loop fusion | flops 3932160 | bytes 11796480 | tf_op jit(solution)/shard_map/stack | solution.py:81
  180.6 12.0 %all_to_all.22 = bf16[2,8,40,6144]{3,2,1,0:T(8,128)(2,1)S(1)} all-to-all(bf16[2,8,40,6144]{3,2,1,0:T(8,128)(2,1)S(1)} %pad_maximum_fusion), channel_id=1, replica_groups=mesh['tok'=8,'tp'=16,'grp'=2] {'grp'}, dimensions={0} | all-to-all | bytes 15728640 | tf_op jit(solution)/shard_map/all_to_all | solution.py:80
  192.6 2.2 fusion.9
  194.8 2.1 copy-done.2
  196.9 0.5 copy-done.6
  197.4 3.0 multiply_convert_fusion.2
  200.5 0.7 copy-done.3
  201.2 5.4 %fusion = bf16[6144,640]{0,1:T(8,128)(2,1)} fusion(bf16[640,256]{1,0:T(8,128)(2,1)S(1)} %get-tuple-element.4, bf16[1,256,6144]{2,1,0:T(8,128)(2,1)S(1)} %copy-done.1), kind=kOutput, calls=%fused_computation.1 | convolution fusion | flops 2017198080 | bytes 11337728 | tf_op jit(solution)/shard_map/dot_general | solution.py:98
  206.6 10.4 %copy.34 = bf16[6144,640]{1,0:T(8,128)(2,1)} copy(bf16[6144,640]{0,1:T(8,128)(2,1)} %fusion) | data formatting | bytes 15728640
  217.1 0.2 reduce-scatter.5.cloned.1.call-start
  217.4 5.6 %fusion.4 = f32[640,256]{1,0:T(8,128)S(1)} fusion(bf16[640,6144]{1,0:T(8,128)(2,1)} %bitcast.54, bf16[1,256,6144]{2,1,0:T(8,128)(2,1)S(1)} %copy-done.1), kind=kOutput, calls=%fused_computation.9 | convolution fusion | flops 2013265920 | bytes 11665408 | tf_op jit(solution)/shard_map/dot_general | solution.py:13
  223.0 0.8 copy-done.9
  223.8 6.2 %fusion.11 = f32[256]{0:T(256)S(1)} fusion(bf16[1,6144,256]{2,1,0:T(8,128)(2,1)S(1)} %copy-done.5, bf16[640,6144]{1,0:T(8,128)(2,1)} %bitcast.58, f32[640,256]{1,0:T(8,128)S(1)} %copy-done.8, f32[640,256]{1,0:T(8,128)S(1)} %fusion.4, f32[640,256]{1,0:T(8,128)S(1)} %copy-done.10), kind=kOutput, calls=%fused_computation.16 | convolution fusion | flops 2021195520 | bytes 12977152 | tf_op jit(solution)/shard_map/dot_general | solution.py:20
  230.1 74.5 %reduce-scatter.7.cloned.1.call-done = bf16[384,640]{1,0:T(8,128)(2,1)} async-done(((bf16[6144,640]{1,0:T(8,128)(2,1)}), bf16[384,640]{1,0:T(8,128)(2,1)}) %reduce-scatter.7.cloned.1.call-update) | async-done | bytes 491536
  304.6 2.0 copy.35
  306.6 7.4 %fusion.12 = f32[256]{0:T(256)S(1)} fusion(bf16[1,6144,256]{2,1,0:T(8,128)(2,1)} %param.16, bf16[640,6144]{1,0:T(8,128)(2,1)} %bitcast.59, f32[640,256]{1,0:T(8,128)} %copy-done.9, f32[640,256]{1,0:T(8,128)} %copy-done.7), kind=kOutput, calls=%fused_computation.17 | convolution fusion | flops 2020540160 | bytes 12321792 | tf_op jit(solution)/shard_map/dot_general | solution.py:23
  314.0 7.7 %reduce-scatter.5.cloned.1.call-done = bf16[384,320]{0,1:T(8,128)(2,1)} async-done(((bf16[384,640]{0,1:T(8,128)(2,1)}), bf16[384,320]{0,1:T(8,128)(2,1)}) %reduce-scatter.5.cloned.1.call-update) | async-done | bytes 245776 | tf_op jit(solution)/shard_map/reduce_scatter | solution.py:105
  321.7 6.5 %all-to-all-start.2 = ((bf16[384,8,40]{0,2,1:T(8,128)(2,1)}), bf16[384,8,40]{0,2,1:T(8,128)(2,1)S(1)}, u32[]{:S(2)}, u32[]{:S(2)}) async-start(bf16[384,8,40]{0,2,1:T(8,128)(2,1)} %bitcast.64), calls=%async_computation.3 | async-start | bytes 491520 | tf_op jit(solution)/shard_map/all_to_all | solution.py:110
  328.1 6.5 %fusion.13 = f32[256]{0:T(256)S(1)} fusion(bf16[1,256,6144]{2,1,0:T(8,128)(2,1)S(1)} %copy-done.1, bf16[640,256]{1,0:T(8,128)(2,1)} %copy-done.3, bf16[640,6144]{1,0:T(8,128)(2,1)} %bitcast.55), kind=kOutput, calls=%fused_computation.18 | convolution fusion | flops 2019557120 | bytes 11338752 | tf_op jit(solution)/shard_map/dot_general | solution.py:26
  334.6 0.6 add_multiply_fusion
  335.2 4.7 %all-to-all-done.2 = bf16[384,8,40]{0,2,1:T(8,128)(2,1)S(1)} async-done(((bf16[384,8,40]{0,2,1:T(8,128)(2,1)}), bf16[384,8,40]{0,2,1:T(8,128)(2,1)S(1)}, u32[]{:S(2)}, u32[]{:S(2)}) %all-to-all-start.2) | async-done | bytes 245792 | tf_op jit(solution)/shard_map/all_to_all | solution.py:110
  339.9 2.0 fusion.15
  (31 shorter events, 0.3 us)
Async XLA Ops:
  7.2 34.2 %copy-start = (bf16[128,384]{1,0:T(8,128)(2,1)S(1)}, bf16[128,384]{1,0:T(8,128)(2,1)}, u32[]{:S(2)}) copy-start(bf16[128,384]{1,0:T(8,128)(2,1)} %param.14) | copy-start | bytes 294916
  7.2 107.0 %all-gather.6.cloned.1.call-start = ((), (), s32[]{:S(2)}) async-start(), calls=%async_computation.8 | async-start | bytes 4177920 | tf_op jit(solution)/shard_map/all_gather | solution.py:75
  56.7 119.9 %all-gather.4.cloned.1.call-start = ((), (), s32[]{:S(2)}) async-start(), calls=%async_computation.6 | async-start | bytes 4177920 | tf_op jit(solution)/shard_map/all_gather | solution.py:74
  105.3 112.0 %all-gather.8.cloned.1.call-start = ((), (), s32[]{:S(2)}) async-start(), calls=%async_computation.9 | async-start | bytes 11796480 | tf_op jit(solution)/shard_map/all_gather | solution.py:88
  114.2 190.4 %reduce-scatter.7.cloned.1.call-start = ((), (), s32[]{:S(2)}) async-start(), calls=%async_computation.10 | async-start | bytes 8355840
  180.6 12.0 %copy-start.4 = (bf16[1,6144,256]{2,1,0:T(8,128)(2,1)S(1)}, bf16[1,6144,256]{2,1,0:T(8,128)(2,1)}, u32[]{:S(2)}) copy-start(bf16[1,6144,256]{2,1,0:T(8,128)(2,1)} %param.15) | copy-start | bytes 9437188
  192.6 4.3 %copy-start.2 = (bf16[2,8,40,6144]{3,2,1,0:T(8,128)(2,1)}, bf16[2,8,40,6144]{3,2,1,0:T(8,128)(2,1)S(1)}, u32[]{:S(2)}) copy-start(bf16[2,8,40,6144]{3,2,1,0:T(8,128)(2,1)S(1)} %all_to_all.22) | copy-start | bytes 23592964
  192.6 4.8 %copy-start.6 = (bf16[1,6144,256]{2,1,0:T(8,128)(2,1)S(1)}, bf16[1,6144,256]{2,1,0:T(8,128)(2,1)}, u32[]{:S(2)}) copy-start(bf16[1,6144,256]{2,1,0:T(8,128)(2,1)} %param.16) | copy-start | bytes 9437188
  197.4 3.0 copy-start.7
  197.4 3.8 %copy-start.1 = (bf16[1,256,6144]{2,1,0:T(8,128)(2,1)S(1)}, bf16[1,256,6144]{2,1,0:T(8,128)(2,1)}, u32[]{:S(2)}) copy-start(bf16[1,256,6144]{2,1,0:T(8,128)(2,1)} %param.17) | copy-start | bytes 9437188
  200.5 0.7 copy-start.3
  217.1 104.6 %reduce-scatter.5.cloned.1.call-start = ((), (), s32[]{:S(2)}) async-start(), calls=%async_computation.7 | async-start | bytes 737280 | tf_op jit(solution)/shard_map/reduce_scatter | solution.py:105
  217.3 6.5 %copy-start.5 = (bf16[1,6144,256]{2,1,0:T(8,128)(2,1)S(1)}, bf16[1,6144,256]{2,1,0:T(8,128)(2,1)}, u32[]{:S(2)}) copy-start(bf16[1,6144,256]{2,1,0:T(8,128)(2,1)} %param.15) | copy-start | bytes 9437188
  217.4 6.5 %copy-start.8 = (f32[640,256]{1,0:T(8,128)S(1)}, f32[640,256]{1,0:T(8,128)}, u32[]{:S(2)}) copy-start(f32[640,256]{1,0:T(8,128)} %copy-done.7) | copy-start | bytes 1966084
  217.4 6.5 %copy-start.10 = (f32[640,256]{1,0:T(8,128)S(1)}, f32[640,256]{1,0:T(8,128)}, u32[]{:S(2)}) copy-start(f32[640,256]{1,0:T(8,128)} %get-tuple-element.5) | copy-start | bytes 1966084
  223.0 0.8 copy-start.9
  321.7 18.3 %all-to-all-start.2 = ((bf16[384,8,40]{0,2,1:T(8,128)(2,1)}), bf16[384,8,40]{0,2,1:T(8,128)(2,1)S(1)}, u32[]{:S(2)}, u32[]{:S(2)}) async-start(bf16[384,8,40]{0,2,1:T(8,128)(2,1)} %bitcast.64), calls=%async_computation.3 | async-start | bytes 491520 | tf_op jit(solution)/shard_map/all_to_all | solution.py:110
Sparse Core Ops, SparseCore 0:
  56.9 57.2 all-gather.5
  116.5 59.9 all-gather.3
  178.4 25.9 all-gather.7
  217.2 87.2 reduce-scatter.6
  306.9 14.6 reduce-scatter.4
